TPU v7x, 128 devices: a whole 4x4x4 slice. The times are simulated.
128 devices in a mesh: pair: 16 (over x, z_lo, core), aux: 8 (over y, z_hi).
Axes of the slice: x: 4, y: 4, z: 4 (z_hi: 2, z_lo: 2; z = z_hi * 2 + z_lo), core: 2. Of those that a mesh axis runs over, the one named last changes fastest.
Arguments:
- integrals: bfloat16 [16, 2, 512, 256, 256], P('pair', None, 'aux'), may hold values from -6 to 6
- coef_table: bfloat16 [2048, 2, 128], P('pair'), may hold values from -0.375 to 0.375
- row_slot: int32 [2048], replicated, may hold values from 0 to 2047, each once
- pair_k: int32 [16, 2], P('pair'), may hold values from 0 to 7, as said below
Outputs:
- exchange_k: float32 [2, 8, 256, 256], P(None, None, 'aux', 'pair')
Inputs may be any that keep to these rules, and one draw needn't show every extreme that they name: `row_slot`: each table row holds exactly one orbital row of one k-point. `pair_k`: the two k-points of a pair differ, and every k-point belongs to some listed pair.
All inputs are finite; a program needn't handle non-finite values.
Results may differ from a plain program's by a relative error of at most 0.0003.
Values may be sent and summed in bfloat16 or wider, within the bound.
A program may use at most 192 MiB of HBM per device.

v0:
```python
import jax
import jax.numpy as jnp
from jax import lax
from jax.sharding import PartitionSpec as P

NKPT = 8


def pick_rows(gathered, row_slot, kpoint, norbitals):
    slots = lax.dynamic_slice_in_dim(row_slot, kpoint * norbitals, norbitals)
    return gathered[slots].reshape(norbitals, -1)


def exchange_block(real_part, imag_part, factor):
    rounded_real = real_part.astype(jnp.bfloat16)
    rounded_imag = imag_part.astype(jnp.bfloat16)
    joined = jnp.concatenate([rounded_real, rounded_imag], -1)
    turned = jnp.concatenate([rounded_imag, -rounded_real], -1)
    k_real = jnp.einsum("pmj,plj->ml", joined, joined, preferred_element_type=jnp.float32)
    k_imag = jnp.einsum("pmj,plj->ml", turned, joined, preferred_element_type=jnp.float32)
    return jnp.stack([k_real, k_imag]) * factor


def local(integrals, coef_table, row_slot, pair_k):
    gathered = lax.all_gather(coef_table, "pair", axis=0, tiled=True)
    norbitals = integrals.shape[-1]
    noccupied = coef_table.shape[-1]
    factor = 1.0 / (integrals.shape[2] * lax.axis_size("aux") * noccupied)
    blocks = integrals[0]
    first_k = pair_k[0, 0]
    second_k = pair_k[0, 1]
    coeff_second = pick_rows(gathered, row_slot, second_k, norbitals)
    coeff_first = pick_rows(gathered, row_slot, first_k, norbitals)
    flat_blocks = blocks.reshape(-1, norbitals)
    product = jnp.dot(flat_blocks, coeff_second, preferred_element_type=jnp.float32)
    product = product.reshape(blocks.shape[:-1] + (2 * noccupied,))
    left_real = product[0, ..., :noccupied] - product[1, ..., noccupied:]
    left_imag = product[0, ..., noccupied:] + product[1, ..., :noccupied]
    first_block = exchange_block(left_real, left_imag, factor)
    product = jnp.einsum("cpmn,mj->cpnj", blocks, coeff_first, preferred_element_type=jnp.float32)
    right_real = product[0, ..., :noccupied] + product[1, ..., noccupied:]
    right_imag = product[0, ..., noccupied:] - product[1, ..., :noccupied]
    second_block = exchange_block(right_real, right_imag, factor)
    kpoints = jnp.arange(NKPT, dtype=jnp.int32)
    first_hot = (kpoints == first_k).astype(jnp.float32)[None, :, None, None]
    second_hot = (kpoints == second_k).astype(jnp.float32)[None, :, None, None]
    spread = first_block[:, None] * first_hot + second_block[:, None] * second_hot
    summed = lax.psum_scatter(spread, "pair", scatter_dimension=3, tiled=True)
    return lax.psum_scatter(summed, "aux", scatter_dimension=2, tiled=True)


def solution(mesh):
    in_specs = (P("pair", None, "aux", None, None), P("pair", None, None), P(), P("pair", None))
    out_specs = P(None, None, "aux", "pair")
    return jax.shard_map(local, mesh=mesh, in_specs=in_specs, out_specs=out_specs, check_vma=False)
```

profile of v0, /device:TPU:0, one launch (start us, length us, event | category | flops | bytes accessed | tf_op | source)
XLA Modules:
  0.0 333.2 jit_solution(5182410068761711925)
XLA Ops:
  6.5 0.7 all-gather.2.cloned.1.call-update
  7.3 0.0 reduce-scatter.5.cloned.1.call-start
  7.3 1.4 fusion.37
  10.0 1.3 compare_convert_fusion
  11.2 0.8 compare_select_fusion.1
  12.0 31.7 %all-gather.2.cloned.1.call-done = bf16[2048,2,128]{2,1,0:T(2,128)(2,1)} async-done(((bf16[128,2,128]{2,1,0:T(2,128)(2,1)}), bf16[2048,2,128]{2,1,0:T(2,128)(2,1)}) %all-gather.2.cloned.1.call-update) | async-done | bytes 1048592 | tf_op jit(solution)/shard_map/all_gather | solution.py:25
  43.7 2.2 gather_fusion.1
  45.9 0.1 copy.32
  46.0 18.9 %convolution_bitcast_fusion.1 = f32[2,64,256,256]{2,3,1,0:T(8,128)} fusion(bf16[256,256,1,1]{0,1,3,2:T(8,128)(2,1)S(1)} %bitcast.55, bf16[1,2,64,256,256]{4,3,2,1,0:T(8,128)(2,1)} %param.4), kind=kOutput, calls=%fused_computation.3 | convolution fusion | flops 4294967296 | bytes 50462720 | tf_op jit(solution)/shard_map/cpmn,mj->cpnj/dot_general | solution.py:40
  64.9 8.8 %fusion.18 = bf16[64,256,128]{1,2,0:T(8,128)(2,1)} fusion(f32[2,64,256,256]{2,3,1,0:T(8,128)} %convolution_bitcast_fusion.1), kind=kLoop, calls=%fused_computation.28 | loop fusion | flops 4194304 | bytes 20971520 | tf_op jit(solution)/shard_map/convert_element_type | solution.py:16
  73.7 9.8 %fusion.35 = (bf16[64,256,128]{1,2,0:T(8,128)(2,1)}, bf16[64,256,128]{1,2,0:T(8,128)(2,1)}) fusion(f32[2,64,256,256]{2,3,1,0:T(8,128)} %convolution_bitcast_fusion.1), kind=kLoop, calls=%fused_computation.49 | loop fusion | flops 6291456 | bytes 25165824 | tf_op jit(solution)/shard_map/neg | solution.py:18
  83.6 2.2 gather_fusion
  85.7 24.4 %convolution_bitcast_fusion = f32[32768,256]{0,1:T(8,128)} fusion(bf16[32768,256]{1,0:T(8,128)(2,1)} %bitcast.51, bf16[32,8,2,128]{3,2,1,0:T(2,128)(2,1)S(1)} %bitcast.53), kind=kOutput, calls=%fused_computation.2 | convolution fusion | flops 4294967296 | bytes 50462720 | tf_op jit(solution)/shard_map/dot_general | solution.py:35
  110.1 33.4 %copy.35 = f32[32768,256]{1,0:T(8,128)} copy(f32[32768,256]{0,1:T(8,128)} %convolution_bitcast_fusion) | data formatting | bytes 67108864 | tf_op jit(solution)/shard_map/reshape | solution.py:36
  143.6 8.6 %fusion.16 = bf16[64,256,128]{2,1,0:T(8,128)(2,1)} fusion(f32[2,64,256,256]{3,2,1,0:T(8,128)} %bitcast.49), kind=kLoop, calls=%fused_computation.26 | loop fusion | flops 4194304 | bytes 20971520 | tf_op jit(solution)/shard_map/convert_element_type | solution.py:16
  152.2 10.0 %fusion.33 = (bf16[64,256,128]{2,1,0:T(8,128)(2,1)}, bf16[64,256,128]{2,1,0:T(8,128)(2,1)}) fusion(f32[2,64,256,256]{3,2,1,0:T(8,128)} %bitcast.50), kind=kLoop, calls=%fused_computation.48 | loop fusion | flops 6291456 | bytes 25165824 | tf_op jit(solution)/shard_map/neg | solution.py:18
  162.2 1.4 copy-done.3
  163.5 2.4 fusion.20
  165.9 2.4 fusion.21
  168.3 0.2 copy.26
  168.6 8.4 %fusion.19 = f32[1,256,256]{2,1,0:T(8,128)S(1)} fusion(bf16[64,256,128]{2,1,0:T(8,128)(2,1)} %fusion.16, bf16[64,256,128]{2,1,0:T(8,128)(2,1)} %get-tuple-element.6), kind=kOutput, calls=%fused_computation.30 | convolution fusion | flops 2164260864 | bytes 8650752 | tf_op jit(solution)/shard_map/pmj,plj->ml/dot_general | solution.py:19
  177.0 1.1 copy-done.5
  178.0 2.4 fusion.24
  180.4 0.2 copy.20
  180.6 2.6 multiply_add_fusion
  183.2 0.0 reduce-scatter.7.cloned.1.call-start
  183.3 68.2 %reduce-scatter.5.cloned.1.call-done = f32[2,8,256,16]{2,3,1,0:T(8,128)} async-done(((f32[2,8,256,256]{2,3,1,0:T(8,128)}), f32[2,8,256,16]{2,3,1,0:T(8,128)}) %reduce-scatter.5.cloned.1.call-update) | async-done | bytes 262160 | tf_op jit(solution)/shard_map/reduce_scatter | solution.py:48
  251.5 2.2 copy.33
  253.8 1.5 reshape.87
  255.3 69.6 %reduce-scatter.7.cloned.1.call-done = f32[32,256]{1,0:T(8,128)} async-done(((f32[256,256]{1,0:T(8,128)}), f32[32,256]{1,0:T(8,128)}) %reduce-scatter.7.cloned.1.call-update) | async-done | bytes 32784
  325.0 0.9 reshape.88
  325.9 0.8 copy.34
  (16 shorter events, 0.1 us)
Async XLA Ops:
  6.5 37.2 %all-gather.2.cloned.1.call-start = ((), (), s32[]{:S(2)}) async-start(), calls=%async_computation.2 | async-start | bytes 1114112 | tf_op jit(solution)/shard_map/all_gather | solution.py:25
  7.3 244.3 %reduce-scatter.5.cloned.1.call-start = ((), (), s32[]{:S(2)}) async-start(), calls=%async_computation.3 | async-start | bytes 4456448 | tf_op jit(solution)/shard_map/reduce_scatter | solution.py:48
  152.2 10.0 %copy-start = (bf16[64,256,128]{1,2,0:T(8,128)(2,1)S(1)}, bf16[64,256,128]{1,2,0:T(8,128)(2,1)}, u32[]{:S(2)}) copy-start(bf16[64,256,128]{1,2,0:T(8,128)(2,1)} %fusion.18) | copy-start | bytes 12582916
  152.2 11.3 %copy-start.3 = (bf16[64,256,128]{1,2,0:T(8,128)(2,1)S(1)}, bf16[64,256,128]{1,2,0:T(8,128)(2,1)}, u32[]{:S(2)}) copy-start(bf16[64,256,128]{1,2,0:T(8,128)(2,1)} %get-tuple-element.8) | copy-start | bytes 12582916
  163.5 2.4 copy-start.2
  168.5 8.4 %copy-start.1 = (bf16[64,256,128]{2,1,0:T(8,128)(2,1)S(1)}, bf16[64,256,128]{2,1,0:T(8,128)(2,1)}, u32[]{:S(2)}) copy-start(bf16[64,256,128]{2,1,0:T(8,128)(2,1)} %fusion.16) | copy-start | bytes 12582916
  168.5 8.4 %copy-start.4 = (bf16[64,256,128]{2,1,0:T(8,128)(2,1)S(1)}, bf16[64,256,128]{2,1,0:T(8,128)(2,1)}, u32[]{:S(2)}) copy-start(bf16[64,256,128]{2,1,0:T(8,128)(2,1)} %get-tuple-element.5) | copy-start | bytes 12582916
  168.5 9.5 %copy-start.5 = (bf16[64,256,128]{2,1,0:T(8,128)(2,1)S(1)}, bf16[64,256,128]{2,1,0:T(8,128)(2,1)}, u32[]{:S(2)}) copy-start(bf16[64,256,128]{2,1,0:T(8,128)(2,1)} %get-tuple-element.6) | copy-start | bytes 12582916
  183.2 141.7 %reduce-scatter.7.cloned.1.call-start = ((), (), s32[]{:S(2)}) async-start(), calls=%async_computation.4 | async-start | bytes 294912
Sparse Core Ops, SparseCore 0:
  9.0 34.6 all-gather.1
  183.4 68.1 reduce-scatter.4
  255.4 69.4 reduce-scatter.6
where the time goes:
time: 334 us; the launch traced here: 333 us
  waiting for transfers between devices  170 us (51%)
  matrix products  58.8 us (18%)
  local copies, waits for them, and re-layouts  47.5 us (14%)
  other arithmetic  41.9 us (13%)
  between operations  14.6 us (4%)
    unnamed x4, waiting for transfers between devices  70.4 us
    reduce_scatter x1, waiting for transfers between devices, local(): summed = lax.psum_scatter(spread, 'pair', scatter_dimension=3, tiled=True)  68.2 us
    reshape x1, local copies, waits for them, and re-layouts, local(): product = product.reshape(blocks.shape[:-1] + (2 * noccupied,))  33.4 us
    all_gather x1, waiting for transfers between devices, local(): gathered = lax.all_gather(coef_table, 'pair', axis=0, tiled=True)  31.7 us
    dot_general x1, matrix products, local(): jnp.dot(flat_blocks, coeff_second, preferred_element_type=jnp.float32)  24.4 us
    neg x2, other arithmetic, exchange_block(): turned = jnp.concatenate([rounded_imag, -rounded_real], -1)  19.8 us
    dot_general x1, matrix products, local(): jnp.einsum('cpmn,mj->cpnj', blocks, coeff_first, preferred_element_type=j...  18.9 us
    convert_element_type x2, other arithmetic, exchange_block(): rounded_imag = imag_part.astype(jnp.bfloat16)  17.4 us
  transfers between devices with their start and end apart: 3, of which 3 were waited for; matrix products, arithmetic and copies ran while one was open for 1% of the time, Pallas kernels for 0%

commit v1 on v0

--- a/solution.py
+++ b/solution.py
@@ -22,7 +22,9 @@
 
 
 def local(integrals, coef_table, row_slot, pair_k):
-    gathered = lax.all_gather(coef_table, "pair", axis=0, tiled=True)
+    gathered = jnp.concatenate(
+        lax.all_to_all(jnp.stack([coef_table] * lax.axis_size("pair")), "pair", 0, 0), axis=0
+    )
     norbitals = integrals.shape[-1]
     noccupied = coef_table.shape[-1]
     factor = 1.0 / (integrals.shape[2] * lax.axis_size("aux") * noccupied)

time: 334 us -> 320 us (0.958)
  waiting for transfers between devices: 170 us -> 150 us
  starting transfers between devices: 0.08 us -> 5.95 us
    all_gather x1 -> x0, waiting for transfers between devices: 31.7 us -> none  [local(): gathered = lax.all_gather(coef_table, 'pair', axis=0, tiled=True)]
    all_to_all x0 -> x1, waiting for transfers between devices: none -> 11.5 us  [local(): lax.all_to_all(jnp.stack([coef_table] * lax.axis_size('pair')), 'pair', 0...]
    all_to_all x0 -> x1, starting transfers between devices: none -> 5.87 us  [local(): lax.all_to_all(jnp.stack([coef_table] * lax.axis_size('pair')), 'pair', 0...]
    unnamed x4 -> x3, waiting for transfers between devices: 70.4 us -> 69.8 us
where the time goes in v1:
time: 320 us; the launch traced here: 319 us
  waiting for transfers between devices  150 us (47%)
  matrix products  58.8 us (18%)
  local copies, waits for them, and re-layouts  47.7 us (15%)
  other arithmetic  42 us (13%)
  between operations  14.9 us (5%)
  starting transfers between devices  5.95 us (2%)
    unnamed x3, waiting for transfers between devices  69.8 us
    reduce_scatter x1, waiting for transfers between devices, local(): summed = lax.psum_scatter(spread, 'pair', scatter_dimension=3, tiled=True)  68.3 us
    reshape x1, local copies, waits for them, and re-layouts, local(): product = product.reshape(blocks.shape[:-1] + (2 * noccupied,))  33.4 us
    dot_general x1, matrix products, local(): jnp.dot(flat_blocks, coeff_second, preferred_element_type=jnp.float32)  24.4 us
    neg x2, other arithmetic, exchange_block(): turned = jnp.concatenate([rounded_imag, -rounded_real], -1)  19.8 us
    dot_general x1, matrix products, local(): jnp.einsum('cpmn,mj->cpnj', blocks, coeff_first, preferred_element_type=j...  19 us
    convert_element_type x2, other arithmetic, exchange_block(): rounded_imag = imag_part.astype(jnp.bfloat16)  17.4 us
    all_to_all x1, waiting for transfers between devices, local(): lax.all_to_all(jnp.stack([coef_table] * lax.axis_size('pair')), 'pair', 0...  11.5 us
  transfers between devices with their start and end apart: 3, of which 3 were waited for; matrix products, arithmetic and copies ran while one was open for 1% of the time, Pallas kernels for 0%

profile of v1, /device:TPU:0, one launch (start us, length us, event | category | flops | bytes accessed | tf_op | source)
XLA Modules:
  0.0 319.0 jit_solution(10913848812313580773)
XLA Ops:
  6.5 2.6 stack.14
  9.2 5.9 %all-to-all-start = ((bf16[16,128,2,128]{3,2,1,0:T(2,128)(2,1)}), bf16[16,128,2,128]{3,2,1,0:T(2,128)(2,1)S(1)}, u32[]{:S(2)}, u32[]{:S(2)}) async-start(bf16[16,128,2,128]{3,2,1,0:T(2,128)(2,1)} %stack.14), calls=%async_computation | async-start | bytes 2097152 | tf_op jit(solution)/shard_map/all_to_all | solution.py:26
  15.0 0.0 reduce-scatter.5.cloned.1.call-start
  15.1 1.4 fusion.37
  17.8 1.3 compare_convert_fusion
  19.2 0.8 compare_select_fusion.1
  20.0 11.5 %all-to-all-done = bf16[16,128,2,128]{3,2,1,0:T(2,128)(2,1)S(1)} async-done(((bf16[16,128,2,128]{3,2,1,0:T(2,128)(2,1)}), bf16[16,128,2,128]{3,2,1,0:T(2,128)(2,1)S(1)}, u32[]{:S(2)}, u32[]{:S(2)}) %all-to-all-start) | async-done | bytes 1048608 | tf_op jit(solution)/shard_map/all_to_all | solution.py:26
  31.5 0.9 gather_fusion.1
  32.4 0.1 copy.42
  32.5 19.0 %convolution_bitcast_fusion.1 = f32[2,64,256,256]{2,3,1,0:T(8,128)} fusion(bf16[256,256,1,1]{0,1,3,2:T(8,128)(2,1)S(1)} %bitcast.58, bf16[1,2,64,256,256]{4,3,2,1,0:T(8,128)(2,1)} %param.4), kind=kOutput, calls=%fused_computation.3 | convolution fusion | flops 4294967296 | bytes 50462720 | tf_op jit(solution)/shard_map/cpmn,mj->cpnj/dot_general | solution.py:42
  51.5 8.8 %fusion.18 = bf16[64,256,128]{1,2,0:T(8,128)(2,1)} fusion(f32[2,64,256,256]{2,3,1,0:T(8,128)} %convolution_bitcast_fusion.1), kind=kLoop, calls=%fused_computation.28 | loop fusion | flops 4194304 | bytes 20971520 | tf_op jit(solution)/shard_map/convert_element_type | solution.py:16
  60.3 9.8 %fusion.35 = (bf16[64,256,128]{1,2,0:T(8,128)(2,1)}, bf16[64,256,128]{1,2,0:T(8,128)(2,1)}) fusion(f32[2,64,256,256]{2,3,1,0:T(8,128)} %convolution_bitcast_fusion.1), kind=kLoop, calls=%fused_computation.49 | loop fusion | flops 6291456 | bytes 25165824 | tf_op jit(solution)/shard_map/neg | solution.py:18
  70.1 0.9 gather_fusion
  71.1 24.4 %convolution_bitcast_fusion = f32[32768,256]{0,1:T(8,128)} fusion(bf16[32768,256]{1,0:T(8,128)(2,1)} %bitcast.52, bf16[32,8,2,128]{3,2,1,0:T(2,128)(2,1)S(1)} %bitcast.56), kind=kOutput, calls=%fused_computation.2 | convolution fusion | flops 4294967296 | bytes 50462720 | tf_op jit(solution)/shard_map/dot_general | solution.py:37
  95.4 33.4 %copy.45 = f32[32768,256]{1,0:T(8,128)} copy(f32[32768,256]{0,1:T(8,128)} %convolution_bitcast_fusion) | data formatting | bytes 67108864 | tf_op jit(solution)/shard_map/reshape | solution.py:38
  128.9 8.6 %fusion.16 = bf16[64,256,128]{2,1,0:T(8,128)(2,1)} fusion(f32[2,64,256,256]{3,2,1,0:T(8,128)} %bitcast.50), kind=kLoop, calls=%fused_computation.26 | loop fusion | flops 4194304 | bytes 20971520 | tf_op jit(solution)/shard_map/convert_element_type | solution.py:16
  137.5 10.0 %fusion.33 = (bf16[64,256,128]{2,1,0:T(8,128)(2,1)}, bf16[64,256,128]{2,1,0:T(8,128)(2,1)}) fusion(f32[2,64,256,256]{3,2,1,0:T(8,128)} %bitcast.51), kind=kLoop, calls=%fused_computation.48 | loop fusion | flops 6291456 | bytes 25165824 | tf_op jit(solution)/shard_map/neg | solution.py:18
  147.5 1.4 copy-done.3
  148.8 2.4 fusion.20
  151.2 2.4 fusion.21
  153.6 0.2 copy.36
  153.9 8.4 %fusion.19 = f32[1,256,256]{2,1,0:T(8,128)S(1)} fusion(bf16[64,256,128]{2,1,0:T(8,128)(2,1)} %fusion.16, bf16[64,256,128]{2,1,0:T(8,128)(2,1)} %get-tuple-element.6), kind=kOutput, calls=%fused_computation.30 | convolution fusion | flops 2164260864 | bytes 8650752 | tf_op jit(solution)/shard_map/pmj,plj->ml/dot_general | solution.py:19
  162.2 1.1 copy-done.5
  163.3 2.4 fusion.24
  165.8 0.2 copy.30
  166.0 2.6 multiply_add_fusion
  168.6 68.3 %reduce-scatter.5.cloned.1.call-done = f32[2,8,256,16]{2,3,1,0:T(8,128)} async-done(((f32[2,8,256,256]{2,3,1,0:T(8,128)}), f32[2,8,256,16]{2,3,1,0:T(8,128)}) %reduce-scatter.5.cloned.1.call-update) | async-done | bytes 262160 | tf_op jit(solution)/shard_map/reduce_scatter | solution.py:50
  236.9 2.2 copy.43
  239.1 1.5 reshape.93
  240.7 69.8 %reduce-scatter.7.cloned.1.call-done = f32[32,256]{1,0:T(8,128)} async-done(((f32[256,256]{1,0:T(8,128)}), f32[32,256]{1,0:T(8,128)}) %reduce-scatter.7.cloned.1.call-update) | async-done | bytes 32784
  310.5 0.9 reshape.94
  311.4 0.8 copy.44
  (16 shorter events, 0.2 us)
Async XLA Ops:
  9.2 22.3 %all-to-all-start = ((bf16[16,128,2,128]{3,2,1,0:T(2,128)(2,1)}), bf16[16,128,2,128]{3,2,1,0:T(2,128)(2,1)S(1)}, u32[]{:S(2)}, u32[]{:S(2)}) async-start(bf16[16,128,2,128]{3,2,1,0:T(2,128)(2,1)} %stack.14), calls=%async_computation | async-start | bytes 2097152 | tf_op jit(solution)/shard_map/all_to_all | solution.py:26
  15.0 221.8 %reduce-scatter.5.cloned.1.call-start = ((), (), s32[]{:S(2)}) async-start(), calls=%async_computation.3 | async-start | bytes 4456448 | tf_op jit(solution)/shard_map/reduce_scatter | solution.py:50
  137.5 10.0 %copy-start = (bf16[64,256,128]{1,2,0:T(8,128)(2,1)S(1)}, bf16[64,256,128]{1,2,0:T(8,128)(2,1)}, u32[]{:S(2)}) copy-start(bf16[64,256,128]{1,2,0:T(8,128)(2,1)} %fusion.18) | copy-start | bytes 12582916
  137.5 11.3 %copy-start.3 = (bf16[64,256,128]{1,2,0:T(8,128)(2,1)S(1)}, bf16[64,256,128]{1,2,0:T(8,128)(2,1)}, u32[]{:S(2)}) copy-start(bf16[64,256,128]{1,2,0:T(8,128)(2,1)} %get-tuple-element.8) | copy-start | bytes 12582916
  148.8 2.4 copy-start.2
  153.8 8.4 %copy-start.1 = (bf16[64,256,128]{2,1,0:T(8,128)(2,1)S(1)}, bf16[64,256,128]{2,1,0:T(8,128)(2,1)}, u32[]{:S(2)}) copy-start(bf16[64,256,128]{2,1,0:T(8,128)(2,1)} %fusion.16) | copy-start | bytes 12582916
  153.8 8.4 %copy-start.4 = (bf16[64,256,128]{2,1,0:T(8,128)(2,1)S(1)}, bf16[64,256,128]{2,1,0:T(8,128)(2,1)}, u32[]{:S(2)}) copy-start(bf16[64,256,128]{2,1,0:T(8,128)(2,1)} %get-tuple-element.5) | copy-start | bytes 12582916
  153.9 9.5 %copy-start.5 = (bf16[64,256,128]{2,1,0:T(8,128)(2,1)S(1)}, bf16[64,256,128]{2,1,0:T(8,128)(2,1)}, u32[]{:S(2)}) copy-start(bf16[64,256,128]{2,1,0:T(8,128)(2,1)} %get-tuple-element.6) | copy-start | bytes 12582916
  168.5 141.9 %reduce-scatter.7.cloned.1.call-start = ((), (), s32[]{:S(2)}) async-start(), calls=%async_computation.4 | async-start | bytes 294912
Sparse Core Ops, SparseCore 0:
  168.7 68.1 reduce-scatter.4
  240.8 69.6 reduce-scatter.6
